TPU v7x, 32 devices: a whole 2x2x4 slice. The times are simulated.
32 devices in a mesh: band: 8 (over z, y), lev: 4 (over x, core).
Axes of the slice: x: 2, y: 2, z: 4, core: 2. Of those that a mesh axis runs over, the one named last changes fastest.
Arguments:
- grid_adjoint: float32 [1024, 64, 2048], P('band', 'lev'), may hold values from -6 to 6
- trajectory: float32 [1024, 64, 2048], P('band', 'lev'), may hold values from -3 to 3
- legendre_north: float32 [512, 512, 512], P(('band', 'lev')), may hold values from -0.25 to 0.25
- slot_wavenumber: int32 [512], replicated, may hold values from 0 to 511, each once
- spectral_state: float32 [512, 512, 2, 64], P(('band', 'lev')), may hold values from -6 to 6
- to_modes: float32 [64, 64], replicated, may hold values from -0.75 to 0.75
- from_modes: float32 [64, 64], replicated, may hold values from -0.75 to 0.75
- rates: float32 [64], replicated, may hold values from 0.1 to 10
Outputs:
- spectral_out: float32 [512, 512, 2, 64], P(('band', 'lev'))
- grid_out: float32 [1024, 64, 2048], P('band', 'lev')
Inputs may be any that keep to these rules, and one draw needn't show every extreme that they name: `slot_wavenumber`: each wavenumber stands in exactly one slot.
All inputs are finite; a program needn't handle non-finite values.
Results may differ from a plain program's by a relative error of at most 0.000067.
Values sent between devices are 32-bit elements; how exact they have to be, the bound alone decides.
A program may use at most 192 MiB of HBM per device.

v0:
```python
import jax
import jax.numpy as jnp
from jax import lax
from jax.sharding import PartitionSpec as P


def wave_table(longitudes, count):
    column = jnp.arange(longitudes, dtype=jnp.int32)
    numbers = jnp.arange(count, dtype=jnp.int32)
    phase = column[:, None] * numbers[None, :] % longitudes
    angles = phase.astype(jnp.float32) * (2.0 * jnp.pi / longitudes)
    scale = jnp.float32(longitudes) ** (-0.5)
    return jnp.concatenate([jnp.cos(angles), -jnp.sin(angles)], axis=1) * scale


def fold(data):
    half = data.shape[2] // 2
    north = data[:, :, :half]
    south = data[:, :, half:][:, :, ::-1]
    return (north + south, north - south)


def by_parity(even_part, odd_part):
    depth_index = jnp.arange(even_part.shape[1], dtype=jnp.int32)
    keep = (depth_index % 2 == 0)[None, :, None, None]
    return jnp.where(keep, even_part, odd_part)


def analyse(north_table, even, odd):
    highest = lax.Precision.HIGHEST
    even_part = jnp.einsum("skt,cstl->skcl", north_table, even, precision=highest)
    odd_part = jnp.einsum("skt,cstl->skcl", north_table, odd, precision=highest)
    return by_parity(even_part, odd_part)


def synthesise(north_table, coeffs):
    highest = lax.Precision.HIGHEST
    depth = north_table.shape[1]
    depth_index = jnp.arange(depth, dtype=jnp.int32)
    even_mask = (depth_index % 2 == 0).astype(jnp.float32)[None, :, None, None]
    even_coeffs = coeffs * even_mask
    odd_coeffs = coeffs - even_coeffs
    first = jnp.einsum("skt,skcl->cstl", north_table, even_coeffs, precision=highest)
    second = jnp.einsum("skt,skcl->cstl", north_table, odd_coeffs, precision=highest)
    north = first + second
    south = (first - second)[:, :, ::-1]
    return jnp.concatenate([north, south], axis=2)


def couple(analysed, state, wavenumbers, to_modes, from_modes, rates):
    highest = lax.Precision.HIGHEST
    depth = analysed.shape[1]
    depth_index = jnp.arange(depth, dtype=jnp.int32)
    valid = (depth_index[None, :] < depth - wavenumbers[:, None]).astype(jnp.float32)
    total = (analysed + state) * valid[:, :, None, None]
    degree = (wavenumbers[:, None] + depth_index[None, :]).astype(jnp.float32)
    helm = degree * (degree + 1.0) / (depth * (depth - 1.0))
    modes = jnp.einsum("skcl,pl->skcp", total, to_modes, precision=highest)
    scaled = modes / (1.0 + helm[:, :, None, None] * rates)
    return jnp.einsum("skcp,lp->skcl", scaled, from_modes, precision=highest)


def shards(
    grid_adjoint,
    trajectory,
    legendre_north,
    slot_wavenumber,
    spectral_state,
    to_modes,
    from_modes,
    rates,
):
    highest = lax.Precision.HIGHEST
    lat_rows, level_rows, longitudes = grid_adjoint.shape
    width = slot_wavenumber.shape[0]
    slot_rows = legendre_north.shape[0]
    bands = lax.axis_size("band")
    levels_count = lax.axis_size("lev")
    band_at = lax.axis_index("band")
    level_at = lax.axis_index("lev")
    table = wave_table(longitudes, width)
    counting = jnp.arange(width, dtype=jnp.int32)
    inverse = jnp.zeros((width,), jnp.int32).at[slot_wavenumber].set(counting)
    forced = grid_adjoint * (1.0 + trajectory)
    flat = forced.reshape(lat_rows * level_rows, longitudes)
    natural = lax.dot_general(
        table, flat, (((0,), (1,)), ((), ())), precision=highest, preferred_element_type=jnp.float32
    )
    natural = natural.reshape(2, width, lat_rows * level_rows)
    fourier = jnp.take(natural, slot_wavenumber, axis=1).reshape(2, width, lat_rows, level_rows)
    own_start = (band_at * levels_count + level_at) * slot_rows
    own_waves = lax.dynamic_slice_in_dim(slot_wavenumber, own_start, slot_rows)
    gathered = lax.all_to_all(
        lax.all_to_all(fourier, "band", split_axis=1, concat_axis=2, tiled=True),
        "lev",
        split_axis=1,
        concat_axis=3,
        tiled=True,
    )
    even, odd = fold(gathered)
    analysed = analyse(legendre_north, even, odd)
    spectral_out = couple(analysed, spectral_state, own_waves, to_modes, from_modes, rates)
    synthesised = synthesise(legendre_north, spectral_out)
    returned = lax.all_to_all(
        lax.all_to_all(synthesised, "band", split_axis=2, concat_axis=1, tiled=True),
        "lev",
        split_axis=3,
        concat_axis=1,
        tiled=True,
    )
    level_part = counting // (bands * slot_rows)
    band_part = counting // slot_rows % bands
    within = counting % slot_rows
    source_slot = band_part * (levels_count * slot_rows) + level_part * slot_rows + within
    arrival_of_slot = jnp.zeros((width,), jnp.int32).at[source_slot].set(counting)
    pick = jnp.take(arrival_of_slot, inverse, axis=0)
    ordered = jnp.take(returned.reshape(2, width, lat_rows * level_rows), pick, axis=1)
    coeff_rows = ordered.reshape(2 * width, lat_rows * level_rows)
    grid_out = lax.dot_general(
        coeff_rows,
        table,
        (((0,), (1,)), ((), ())),
        precision=highest,
        preferred_element_type=jnp.float32,
    )
    return (spectral_out, grid_out.reshape(lat_rows, level_rows, longitudes))


def solution(mesh):
    return jax.shard_map(
        shards,
        mesh=mesh,
        in_specs=(
            P("band", "lev", None),
            P("band", "lev", None),
            P(("band", "lev"), None, None),
            P(),
            P(("band", "lev"), None, None, None),
            P(),
            P(),
            P(),
        ),
        out_specs=(P(("band", "lev"), None, None, None), P("band", "lev", None)),
        check_vma=False,
    )
```

profile of v0, /device:TPU:0, one launch (start us, length us, event | category | flops | bytes accessed | tf_op | source)
XLA Modules:
  0.0 1142.6 jit_solution(12280588452169938446)
XLA Ops:
  0.7 16.5 %sine_negate_fusion = (f32[2048,512]{1,0:T(8,128)S(1)}, f32[2048,512]{1,0:T(8,128)S(1)}) fusion(), kind=kLoop, calls=%fused_computation.41 | loop fusion | flops 15728640 | bytes 8388608 | tf_op jit(solution)/shard_map/neg | solution.py:13
  17.2 1.9 copy-done.4
  20.4 4.9 fusion.10
  25.3 9.2 copy.79
  34.5 11.7 %add_multiply_fusion = f32[128,16,2048]{2,1,0:T(8,128)S(1)} fusion(f32[128,16,2048]{2,1,0:T(8,128)} %param.10, f32[128,16,2048]{2,1,0:T(8,128)} %param.11), kind=kLoop, calls=%fused_computation.13 | loop fusion | flops 8388608 | bytes 50331648 | tf_op jit(solution)/shard_map/mul | solution.py:84
  46.2 66.8 %fusion.57 = f32[2,512,2048]{2,1,0:T(8,128)} fusion(f32[2,512,2048]{2,1,0:T(8,128)} %bitcast.91, f32[2048,2048,1]{1,0,2:T(8,128)S(1)} %bitcast.89), kind=kOutput, calls=%fused_computation.99 | convolution fusion | flops 51539607552 | bytes 33554432 | tf_op jit(solution)/shard_map/dot_general | solution.py:86
  113.0 15.4 %copy.80 = f32[2,512,2048]{2,0,1:T(2,128)} copy(f32[2,512,2048]{2,1,0:T(8,128)} %fusion.57) | data formatting | bytes 16777216 | tf_op jit(solution)/shard_map/dot_general | solution.py:86
  128.5 22.7 %gather_fusion.1 = f32[512,2,2048]{2,1,0:T(2,128)} fusion(f32[2,512,2048]{2,0,1:T(2,128)} %copy.80, s32[1024]{0:T(1024)S(1)} %pad_clamp_fusion.2), kind=kCustom, calls=%fused_computation.clone | custom fusion | bytes 16779264 | tf_op jit(solution)/shard_map/jit(_take)/gather | solution.py:90
  151.2 8.5 select_bitcast_fusion.1
  159.7 13.1 %copy.81 = f32[2,512,2048]{1,2,0:T(8,128)} copy(f32[2,512,2048]{2,0,1:T(2,128)} %select_bitcast_fusion.1) | data formatting | bytes 16777216 | tf_op jit(solution)/shard_map/jit(_take)/select_n | solution.py:90
  172.8 10.8 copy.82
  183.6 190.4 %all_to_all.69 = f32[2,512,128,16]{2,3,0,1:T(8,128)S(1)} all-to-all(f32[2,512,128,16]{2,3,0,1:T(8,128)} %copy.82), channel_id=1, replica_groups=mesh['band'=8,'lev'=4] {'band'}, dimensions={1} | all-to-all | bytes 16777216 | tf_op jit(solution)/shard_map/all_to_all | solution.py:94
  373.9 4.6 copy.120
  378.5 6.2 all-to-all-start.1
  384.9 1.7 multiply_add_fusion
  386.7 91.2 %all-to-all-done.1 = f32[2,64,1024,16]{2,3,0,1:T(8,128)} async-done(((f32[2,64,1024,16]{2,3,0,1:T(8,128)}), f32[2,64,1024,16]{2,3,0,1:T(8,128)}, u32[]{:S(2)}, u32[]{:S(2)}) %all-to-all-start.1) | async-done | bytes 8388640 | tf_op jit(solution)/shard_map/all_to_all | solution.py:93
  477.8 4.2 copy.87
  482.1 3.4 copy-done.2
  485.4 2.5 slice.15
  487.9 7.4 rev.6
  495.4 4.7 slice_subtract_fusion
  500.0 21.0 %fusion.4 = f32[16,2,64,512]{3,2,1,0:T(8,128)S(1)} fusion(f32[16,512,512]{2,1,0:T(8,128)} %param.12, f32[2,16,512,64]{2,3,1,0:T(8,128)S(1)} %get-tuple-element.19), kind=kOutput, calls=%fused_computation.9 | convolution fusion | flops 6442450944 | bytes 25165824 | tf_op jit(solution)/shard_map/skt,cstl->skcl/dot_general | solution.py:32
  521.0 21.4 %fusion.6 = f32[16,2,64,512]{3,2,1,0:T(8,128)S(1)} fusion(f32[16,512,512]{2,1,0:T(8,128)} %param.12, f32[2,16,512,64]{2,3,1,0:T(8,128)S(1)} %get-tuple-element.20), kind=kOutput, calls=%fused_computation.11 | convolution fusion | flops 6442450944 | bytes 25165824 | tf_op jit(solution)/shard_map/skt,cstl->skcl/dot_general | solution.py:31
  542.5 7.9 fusion.16
  550.4 5.0 fusion.20
  555.4 16.0 %fusion = f32[16,2,64,512]{3,2,1,0:T(8,128)} fusion(f32[16,512,512]{2,1,0:T(8,128)} %param.12, f32[16,512,2,64]{1,3,2,0:T(8,128)S(1)} %fusion.20, f32[512]{0:T(512)S(1)} %fusion.50), kind=kOutput, calls=%fused_computation.5 | convolution fusion | flops 6444548096 | bytes 25167872 | tf_op jit(solution)/shard_map/skt,skcl->cstl/dot_general | solution.py:44
  571.4 15.8 %add_bitcast_fusion = (f32[2,16,512,64]{2,3,0,1:T(8,128)}, f32[2,16,512,64]{2,3,0,1:T(8,128)}) fusion(f32[16,2,64,512]{3,2,1,0:T(8,128)} %fusion, f32[16,512,512]{2,1,0:T(8,128)} %param.12, f32[16,512,2,64]{1,3,2,0:T(8,128)S(1)} %fusion.20, f32[512]{0:T(512)S(1)} %fusion.50), kind=kOutput, calls=%fused_computation.36 | convolution fusion | flops 6445596672 | bytes 33556480 | tf_op jit(solution)/shard_map/skt,skcl->cstl/dot_general | solution.py:43
  587.3 7.4 rev.7
  594.7 8.1 pad_maximum_fusion
  602.8 23.1 %copy.90 = f32[2,16,1024,64]{3,0,1,2:T(2,128)} copy(f32[2,16,1024,64]{2,3,0,1:T(8,128)} %pad_maximum_fusion) | data formatting | bytes 16777216 | tf_op jit(solution)/shard_map/concatenate | solution.py:47
  625.9 20.1 %reshape.290 = f32[8,1,262144]{2,1,0:T(1,128)} reshape(f32[1024,16,2,64]{3,2,1,0:T(2,128)} %bitcast.80) | data formatting | bytes 16777216
  646.1 188.7 %all_to_all.70 = f32[8,1,262144]{2,1,0:T(1,128)} all-to-all(f32[8,1,262144]{2,1,0:T(1,128)} %reshape.290), channel_id=1, replica_groups=mesh['band'=8,'lev'=4] {'band'}, dimensions={0} | all-to-all | bytes 16777216 | tf_op jit(solution)/shard_map/all_to_all | solution.py:105
  835.3 26.4 %reduce = f32[8,262144]{1,0:T(8,128)} reduce(f32[8,1,262144]{2,1,0:T(1,128)} %all_to_all.70, f32[]{:T(128)} %broadcast.326), dimensions={1}, to_apply=%all_to_all.58.reduce_sub_computation | reduce | bytes 16777220 | tf_op jit(solution)/shard_map/all_to_all | solution.py:105
  861.7 25.7 %reshape.291 = f32[1024,16,2,64]{3,2,1,0:T(2,128)} reshape(f32[8,262144]{1,0:T(8,128)} %reduce) | data formatting | bytes 16777216
  887.5 17.4 %copy.111 = f32[2,16,8,128,64]{3,1,2,0,4:T(8,128)} copy(f32[2,16,8,128,64]{4,0,1,3,2:T(2,128)} %bitcast.81) | data formatting | bytes 16777216 | tf_op jit(solution)/shard_map/all_to_all | solution.py:105
  904.8 5.6 all-to-all-start.3
  910.5 2.4 scatter_custom_fusion
  913.0 2.4 scatter_custom_fusion.1
  915.4 3.5 gather_fusion
  919.0 84.7 %all-to-all-done.3 = f32[2,128,128,64]{2,1,0,3:T(8,128)} async-done(((f32[2,128,128,64]{2,1,0,3:T(8,128)}), f32[2,128,128,64]{2,1,0,3:T(8,128)}, u32[]{:S(2)}, u32[]{:S(2)}) %all-to-all-start.3) | async-done | bytes 8388640 | tf_op jit(solution)/shard_map/all_to_all | solution.py:104
  1003.6 10.3 copy.95
  1013.9 10.3 reshape.230
  1024.2 13.3 %copy.96 = f32[2,512,2048]{2,0,1:T(2,128)} copy(f32[2,512,2048]{1,2,0:T(8,128)} %reshape.230) | data formatting | bytes 16777216 | tf_op jit(solution)/shard_map/reshape | solution.py:117
  1037.5 22.7 %gather_fusion.2 = f32[512,2,2048]{2,1,0:T(2,128)} fusion(f32[2,512,2048]{2,0,1:T(2,128)} %copy.96, s32[1024]{0:T(1024)S(1)} %pad_clamp_fusion), kind=kCustom, calls=%fused_computation.1.clone | custom fusion | bytes 16779264 | tf_op jit(solution)/shard_map/jit(_take)/gather | solution.py:117
  1060.2 6.4 select_bitcast_fusion
  1066.6 8.3 copy.97
  1074.8 9.3 copy.98
  1084.1 58.1 %fusion.8 = f32[128,16,2048]{2,1,0:T(8,128)} fusion(f32[128,16,1024]{2,1,0:T(8,128)} %bitcast.90, f32[2048,512]{1,0:T(8,128)} %copy-done.4, f32[2048,512]{1,0:T(8,128)} %copy-done.5), kind=kOutput, calls=%fused_computation.17 | convolution fusion | flops 51543801856 | bytes 33554432 | tf_op jit(solution)/shard_map/dot_general | solution.py:119
  (34 shorter events, 2.1 us)
Async XLA Ops:
  0.6 541.8 %copy-start = (f32[64,64]{1,0:T(8,128)S(1)}, f32[64,64]{1,0:T(8,128)}, u32[]{:S(2)}) copy-start(f32[64,64]{1,0:T(8,128)} %param.15) | copy-start | bytes 49156
  0.6 16.5 %copy-start.7 = (s32[512]{0:T(512)S(1)}, s32[512]{0:T(512)}, u32[]{:S(2)}) copy-start(s32[512]{0:T(512)} %param.13) | copy-start | bytes 6148
  17.2 1.9 copy-start.4
  17.2 3.2 copy-start.5
  378.5 6.4 copy-start.8
  378.5 99.3 %all-to-all-start.1 = ((f32[2,64,1024,16]{2,3,0,1:T(8,128)}), f32[2,64,1024,16]{2,3,0,1:T(8,128)}, u32[]{:S(2)}, u32[]{:S(2)}) async-start(f32[2,64,1024,16]{2,3,0,1:T(8,128)} %bitcast.83), calls=%async_computation.1 | async-start | bytes 16777216 | tf_op jit(solution)/shard_map/all_to_all | solution.py:93
  482.0 3.4 copy-start.2
  542.4 7.9 copy-start.6
  542.4 7.9 copy-start.9
  555.4 16.0 %copy-start.3 = (f32[16,512,2,64]{1,3,2,0:T(8,128)}, f32[16,512,2,64]{1,3,2,0:T(8,128)S(1)}, u32[]{:S(2)}) copy-start(f32[16,512,2,64]{1,3,2,0:T(8,128)S(1)} %fusion.20) | copy-start | bytes 12582916
  904.8 98.8 %all-to-all-start.3 = ((f32[2,128,128,64]{2,1,0,3:T(8,128)}), f32[2,128,128,64]{2,1,0,3:T(8,128)}, u32[]{:S(2)}, u32[]{:S(2)}) async-start(f32[2,128,128,64]{2,1,0,3:T(8,128)} %bitcast.82), calls=%async_computation.3 | async-start | bytes 16777216 | tf_op jit(solution)/shard_map/all_to_all | solution.py:104
  1084.1 58.1 %copy-start.1 = (f32[64,64]{1,0:T(8,128)S(1)}, f32[64,64]{1,0:T(8,128)}, u32[]{:S(2)}) copy-start(f32[64,64]{1,0:T(8,128)} %param.15) | copy-start | bytes 49156
where the time goes:
time: 1150 us; the launch traced here: 1140 us
  blocking collectives  379 us (33%)
  local copies, waits for them, and re-layouts  273 us (24%)
  matrix products  212 us (18%)
  waiting for transfers between devices  176 us (15%)
  other arithmetic  89.2 us (8%)
  starting transfers between devices  11.8 us (1%)
    all_to_all x1, blocking collectives, shards(): lax.all_to_all(fourier, 'band', split_axis=1, concat_axis=2, tiled=True)  190 us
    all_to_all x1, blocking collectives, shards(): lax.all_to_all(synthesised, 'band', split_axis=2, concat_axis=1, tiled=True)  189 us
    all_to_all x1, waiting for transfers between devices, shards(): lax.all_to_all(lax.all_to_all(fourier, 'band', split_axis=1, concat_axis=...  91.2 us
    all_to_all x1, waiting for transfers between devices, shards(): lax.all_to_all(lax.all_to_all(synthesised, 'band', split_axis=2, concat_a...  84.7 us
    dot_general x1, matrix products, shards(): lax.dot_general(table, flat, (((0,), (1,)), ((), ())), precision=highest,...  66.8 us
    dot_general x1, matrix products, shards(): lax.dot_general(coeff_rows, table, (((0,), (1,)), ((), ())), precision=hi...  58.1 us
    unnamed x22, local copies, waits for them, and re-layouts  52.5 us
    all_to_all x1, other arithmetic, shards(): lax.all_to_all(synthesised, 'band', split_axis=2, concat_axis=1, tiled=True)  26.4 us
  transfers between devices with their start and end apart: 2, of which 2 were waited for; matrix products, arithmetic and copies ran while one was open for 1% of the time, Pallas kernels for 0%

commit v1 on v0

--- a/solution.py
+++ b/solution.py
@@ -91,7 +91,12 @@
     own_start = (band_at * levels_count + level_at) * slot_rows
     own_waves = lax.dynamic_slice_in_dim(slot_wavenumber, own_start, slot_rows)
     gathered = lax.all_to_all(
-        lax.all_to_all(fourier, "band", split_axis=1, concat_axis=2, tiled=True),
+        jnp.concatenate(
+            lax.all_to_all(
+                jnp.stack(jnp.split(fourier, lax.axis_size("band"), axis=1)), "band", 0, 0
+            ),
+            axis=2,
+        ),
         "lev",
         split_axis=1,
         concat_axis=3,

time: 1150 us -> 1200 us (1.043)
  blocking collectives: 379 us -> 480 us
  waiting for transfers between devices: 176 us -> 91.2 us
  local copies, waits for them, and re-layouts: 273 us -> 304 us
    all_to_all x1 -> x2, blocking collectives: 190 us -> 291 us  [the longest x1 191 us: shards(): lax.all_to_all(jnp.stack(jnp.split(fourier, lax.axis_size('band'), axis=1...]
    all_to_all x2 -> x1, waiting for transfers between devices: 176 us -> 91.2 us  [shards(): lax.all_to_all(jnp.concatenate(lax.all_to_all(jnp.stack(jnp.split(fourier...]
    another operation x0 -> x2, local copies, waits for them, and re-layouts: none -> 15.7 us  [shards(): jnp.stack(jnp.split(fourier, lax.axis_size('band'), axis=1))]
    unnamed x22 -> x31, local copies, waits for them, and re-layouts: 52.5 us -> 65.3 us
  transfers between devices with their start and end apart: 2 -> 1, of which waited for: 2 -> 1; matrix products, arithmetic and copies ran while one was open for 1% -> 0% of each run, Pallas kernels for 0% -> 0%
where the time goes in v1:
time: 1200 us; the launch traced here: 1190 us
  blocking collectives  480 us (40%)
  local copies, waits for them, and re-layouts  304 us (25%)
  matrix products  212 us (18%)
  other arithmetic  95.4 us (8%)
  waiting for transfers between devices  91.2 us (8%)
    all_to_all x1, blocking collectives, shards(): lax.all_to_all(jnp.stack(jnp.split(fourier, lax.axis_size('band'), axis=1...  191 us
    all_to_all x1, blocking collectives, shards(): lax.all_to_all(synthesised, 'band', split_axis=2, concat_axis=1, tiled=True)  189 us
    all_to_all x1, blocking collectives, shards(): lax.all_to_all(lax.all_to_all(synthesised, 'band', split_axis=2, concat_a...  101 us
    all_to_all x1, waiting for transfers between devices, shards(): lax.all_to_all(jnp.concatenate(lax.all_to_all(jnp.stack(jnp.split(fourier...  91.2 us
    dot_general x1, matrix products, shards(): lax.dot_general(table, flat, (((0,), (1,)), ((), ())), precision=highest,...  67 us
    unnamed x31, local copies, waits for them, and re-layouts  65.3 us
    dot_general x1, matrix products, shards(): lax.dot_general(coeff_rows, table, (((0,), (1,)), ((), ())), precision=hi...  58 us
    all_to_all x1, other arithmetic, shards(): lax.all_to_all(synthesised, 'band', split_axis=2, concat_axis=1, tiled=True)  26.7 us
  transfers between devices with their start and end apart: 1, of which 1 were waited for; matrix products, arithmetic and copies ran while one was open for 0% of the time, Pallas kernels for 0%

profile of v1, /device:TPU:0, one launch (start us, length us, event | category | flops | bytes accessed | tf_op | source)
XLA Modules:
  0.0 1189.8 jit_solution(4107594151273985878)
XLA Ops:
  0.7 17.7 %sine_negate_fusion = (f32[2048,512]{1,0:T(8,128)}, f32[2048,512]{1,0:T(8,128)}) fusion(), kind=kLoop, calls=%fused_computation.40 | loop fusion | flops 15728640 | bytes 8388608 | tf_op jit(solution)/shard_map/neg | solution.py:13
  18.4 2.4 scatter_custom_fusion
  20.9 2.4 scatter_custom_fusion.1
  23.4 3.5 gather_fusion
  28.0 8.6 fusion.10
  36.6 9.2 copy.41
  45.8 11.7 add_multiply_fusion
  57.5 67.0 %fusion.65 = f32[2,512,2048]{2,1,0:T(8,128)} fusion(f32[2,512,2048]{2,1,0:T(8,128)} %bitcast.128, f32[2048,2048,1]{1,0,2:T(8,128)S(1)} %bitcast.126), kind=kOutput, calls=%fused_computation.114 | convolution fusion | flops 51539607552 | bytes 33554432 | tf_op jit(solution)/shard_map/dot_general | solution.py:86
  124.5 15.4 %copy.42 = f32[2,512,2048]{2,0,1:T(2,128)} copy(f32[2,512,2048]{2,1,0:T(8,128)} %fusion.65) | data formatting | bytes 16777216 | tf_op jit(solution)/shard_map/dot_general | solution.py:86
  140.0 22.7 %gather_fusion.1 = f32[512,2,2048]{2,1,0:T(2,128)} fusion(f32[2,512,2048]{2,0,1:T(2,128)} %copy.42, s32[1024]{0:T(1024)S(1)} %get-tuple-element.22), kind=kCustom, calls=%fused_computation.clone | custom fusion | bytes 16779264 | tf_op jit(solution)/shard_map/jit(_take)/gather | solution.py:90
  162.7 8.5 select_bitcast_fusion.1
  171.1 13.1 %copy.43 = f32[2,512,2048]{1,2,0:T(8,128)} copy(f32[2,512,2048]{2,0,1:T(2,128)} %select_bitcast_fusion.1) | data formatting | bytes 16777216 | tf_op jit(solution)/shard_map/jit(_take)/select_n | solution.py:90
  184.3 3.2 fusion.34
  187.5 4.1 fusion.33
  202.2 13.8 %copy.44 = f32[8,2,64,128,16]{3,4,2,1,0:T(8,128)} copy(f32[8,2,64,128,16]{2,4,3,1,0:T(8,128)} %fusion.27) | data formatting | bytes 16777216 | tf_op jit(solution)/shard_map/stack | solution.py:96
  216.0 190.5 %all_to_all.56 = f32[8,2,64,128,16]{3,4,2,1,0:T(8,128)S(1)} all-to-all(f32[8,2,64,128,16]{3,4,2,1,0:T(8,128)} %copy.44), channel_id=1, replica_groups=mesh['band'=8,'lev'=4] {'band'}, dimensions={0} | all-to-all | bytes 16777216 | tf_op jit(solution)/shard_map/all_to_all | solution.py:95
  406.5 8.3 copy.67
  414.8 9.3 reshape.293
  424.0 5.8 all-to-all-start.1
  431.8 91.2 %all-to-all-done.1 = f32[2,64,1024,16]{2,3,0,1:T(8,128)} async-done(((f32[2,64,1024,16]{2,3,0,1:T(8,128)}), f32[2,64,1024,16]{2,3,0,1:T(8,128)}, u32[]{:S(2)}, u32[]{:S(2)}) %all-to-all-start.1) | async-done | bytes 8388640 | tf_op jit(solution)/shard_map/all_to_all | solution.py:93
  522.9 4.2 copy.48
  527.2 3.4 copy-done.3
  530.6 2.5 slice.15
  533.1 7.4 rev.6
  540.5 4.7 slice_subtract_fusion
  545.2 21.0 %fusion.4 = f32[16,2,64,512]{3,2,1,0:T(8,128)S(1)} fusion(f32[16,512,512]{2,1,0:T(8,128)} %param.12, f32[2,16,512,64]{2,3,1,0:T(8,128)S(1)} %get-tuple-element.15), kind=kOutput, calls=%fused_computation.9 | convolution fusion | flops 6442450944 | bytes 25165824 | tf_op jit(solution)/shard_map/skt,cstl->skcl/dot_general | solution.py:32
  566.2 21.6 %fusion.6 = f32[16,2,64,512]{3,2,1,0:T(8,128)S(1)} fusion(f32[16,512,512]{2,1,0:T(8,128)} %param.12, f32[2,16,512,64]{2,3,1,0:T(8,128)S(1)} %get-tuple-element.16), kind=kOutput, calls=%fused_computation.11 | convolution fusion | flops 6442450944 | bytes 25165824 | tf_op jit(solution)/shard_map/skt,cstl->skcl/dot_general | solution.py:31
  587.8 7.9 fusion.16
  595.7 5.0 fusion.20
  600.8 16.0 %fusion = f32[16,2,64,512]{3,2,1,0:T(8,128)} fusion(f32[16,512,512]{2,1,0:T(8,128)} %param.12, f32[16,512,2,64]{1,3,2,0:T(8,128)S(1)} %fusion.20, f32[512]{0:T(512)S(1)} %fusion.58), kind=kOutput, calls=%fused_computation.5 | convolution fusion | flops 6444548096 | bytes 25167872 | tf_op jit(solution)/shard_map/skt,skcl->cstl/dot_general | solution.py:44
  616.8 15.8 %add_bitcast_fusion = (f32[2,16,512,64]{2,3,0,1:T(8,128)}, f32[2,16,512,64]{2,3,0,1:T(8,128)}) fusion(f32[16,2,64,512]{3,2,1,0:T(8,128)} %fusion, f32[16,512,512]{2,1,0:T(8,128)} %param.12, f32[16,512,2,64]{1,3,2,0:T(8,128)S(1)} %fusion.20, f32[512]{0:T(512)S(1)} %fusion.58), kind=kOutput, calls=%fused_computation.35 | convolution fusion | flops 6445596672 | bytes 33556480 | tf_op jit(solution)/shard_map/skt,skcl->cstl/dot_general | solution.py:43
  632.7 7.4 rev.7
  640.1 8.1 pad_maximum_fusion
  648.2 23.1 %copy.51 = f32[2,16,1024,64]{3,0,1,2:T(2,128)} copy(f32[2,16,1024,64]{2,3,0,1:T(8,128)} %pad_maximum_fusion) | data formatting | bytes 16777216 | tf_op jit(solution)/shard_map/concatenate | solution.py:47
  671.3 20.1 %reshape.298 = f32[8,1,262144]{2,1,0:T(1,128)} reshape(f32[1024,16,2,64]{3,2,1,0:T(2,128)} %bitcast.118) | data formatting | bytes 16777216
  691.4 188.7 %all_to_all.57 = f32[8,1,262144]{2,1,0:T(1,128)} all-to-all(f32[8,1,262144]{2,1,0:T(1,128)} %reshape.298), channel_id=1, replica_groups=mesh['band'=8,'lev'=4] {'band'}, dimensions={0} | all-to-all | bytes 16777216 | tf_op jit(solution)/shard_map/all_to_all | solution.py:110
  880.7 26.7 %reduce = f32[8,262144]{1,0:T(8,128)} reduce(f32[8,1,262144]{2,1,0:T(1,128)} %all_to_all.57, f32[]{:T(128)} %broadcast.326), dimensions={1}, to_apply=%all_to_all.45.reduce_sub_computation | reduce | bytes 16777220 | tf_op jit(solution)/shard_map/all_to_all | solution.py:110
  907.3 25.7 %reshape.299 = f32[1024,16,2,64]{3,2,1,0:T(2,128)} reshape(f32[8,262144]{1,0:T(8,128)} %reduce) | data formatting | bytes 16777216
  933.1 17.4 %copy.71 = f32[2,16,8,128,64]{3,1,2,0,4:T(8,128)} copy(f32[2,16,8,128,64]{4,0,1,3,2:T(2,128)} %bitcast.119) | data formatting | bytes 16777216 | tf_op jit(solution)/shard_map/all_to_all | solution.py:110
  950.5 100.6 %all_to_all.58 = f32[2,128,128,64]{2,1,0,3:T(8,128)} all-to-all(f32[2,128,128,64]{2,1,0,3:T(8,128)} %bitcast.120), channel_id=1, replica_groups=mesh['band'=8,'lev'=4] {'lev'}, dimensions={3} | all-to-all | bytes 16777216 | tf_op jit(solution)/shard_map/all_to_all | solution.py:109
  1051.0 10.3 copy.56
  1061.3 10.3 reshape.238
  1071.6 13.3 %copy.57 = f32[2,512,2048]{2,0,1:T(2,128)} copy(f32[2,512,2048]{1,2,0:T(8,128)} %reshape.238) | data formatting | bytes 16777216 | tf_op jit(solution)/shard_map/reshape | solution.py:122
  1084.9 22.7 %gather_fusion.2 = f32[512,2,2048]{2,1,0:T(2,128)} fusion(f32[2,512,2048]{2,0,1:T(2,128)} %copy.57, s32[1024]{0:T(1024)S(1)} %copy-done.7), kind=kCustom, calls=%fused_computation.1.clone | custom fusion | bytes 16779264 | tf_op jit(solution)/shard_map/jit(_take)/gather | solution.py:122
  1107.6 6.4 select_bitcast_fusion
  1114.0 8.3 copy.58
  1122.2 9.3 copy.59
  1131.5 58.0 %fusion.8 = f32[128,16,2048]{2,1,0:T(8,128)} fusion(f32[128,16,1024]{2,1,0:T(8,128)} %bitcast.127, f32[2048,512]{1,0:T(8,128)} %get-tuple-element.19, f32[2048,512]{1,0:T(8,128)} %get-tuple-element.20), kind=kOutput, calls=%fused_computation.16 | convolution fusion | flops 51543801856 | bytes 33554432 | tf_op jit(solution)/shard_map/dot_general | solution.py:124
  (43 shorter events, 14.3 us)
Async XLA Ops:
  0.6 587.2 %copy-start = (f32[64,64]{1,0:T(8,128)S(1)}, f32[64,64]{1,0:T(8,128)}, u32[]{:S(2)}) copy-start(f32[64,64]{1,0:T(8,128)} %param.15) | copy-start | bytes 49156
  0.6 17.7 %copy-start.6 = (s32[512]{0:T(512)S(1)}, s32[512]{0:T(512)}, u32[]{:S(2)}) copy-start(s32[512]{0:T(512)} %param.13) | copy-start | bytes 6148
  184.3 7.3 copy-start.2
  424.0 6.0 copy-start.9
  424.0 98.9 %all-to-all-start.1 = ((f32[2,64,1024,16]{2,3,0,1:T(8,128)}), f32[2,64,1024,16]{2,3,0,1:T(8,128)}, u32[]{:S(2)}, u32[]{:S(2)}) async-start(f32[2,64,1024,16]{2,3,0,1:T(8,128)} %reshape.293), calls=%async_computation.1 | async-start | bytes 16777216 | tf_op jit(solution)/shard_map/all_to_all | solution.py:93
  527.2 3.4 copy-start.3
  587.8 7.9 copy-start.5
  587.8 7.9 copy-start.10
  600.8 16.1 %copy-start.4 = (f32[16,512,2,64]{1,3,2,0:T(8,128)}, f32[16,512,2,64]{1,3,2,0:T(8,128)S(1)}, u32[]{:S(2)}) copy-start(f32[16,512,2,64]{1,3,2,0:T(8,128)S(1)} %fusion.20) | copy-start | bytes 12582916
  1071.6 13.3 %copy-start.7 = (s32[1024]{0:T(1024)S(1)}, s32[1024]{0:T(1024)}, u32[]{:S(2)}) copy-start(s32[1024]{0:T(1024)} %get-tuple-element.21) | copy-start | bytes 12292
  1084.9 22.7 %copy-start.8 = (pred[512]{0:T(512)(128)(4,1)S(1)}, pred[512]{0:T(512)(128)(4,1)}, u32[]{:S(2)}) copy-start(pred[512]{0:T(512)(128)(4,1)} %get-tuple-element.11) | copy-start | bytes 1540
  1131.5 58.0 %copy-start.1 = (f32[64,64]{1,0:T(8,128)S(1)}, f32[64,64]{1,0:T(8,128)}, u32[]{:S(2)}) copy-start(f32[64,64]{1,0:T(8,128)} %param.15) | copy-start | bytes 49156
